TPU v7x, 256 devices: a whole 4x4x8 slice. The times are simulated.
256 devices in a mesh: dp: 16 (over x, y), head: 16 (over z, core).
Axes of the slice: x: 4, y: 4, z: 8, core: 2. Of those that a mesh axis runs over, the one named last changes fastest.
Arguments:
- latents: bfloat16 [2048, 512], P('dp'), may hold values from -6 to 6
- targets: bfloat16 [2048, 32768], P('dp', 'head'), may hold values from -6 to 6
- kv_weight: bfloat16 [512, 32768], P(None, 'head'), may hold values from -0.25 to 0.25
- momentum: float32 [512, 16, 2048], P(None, 'head', 'dp'), may hold values from -120 to 120
Outputs:
- momentum_out: float32 [512, 16, 2048], P(None, 'head', 'dp')
- update: float32 [512, 16, 2048], P(None, 'head', 'dp')
All inputs are finite; a program needn't handle non-finite values.
Results may differ from a plain program's by a relative error of at most 0.0003.
The roundings to bfloat16 on the way count: a program that leaves them out, or rounds other values in their place, can miss the bound.
Values may be sent and summed in bfloat16 or wider, within the bound.
A program may use at most 64 MiB of HBM per device.

v0:
```python
import math

import jax
import jax.numpy as jnp
from jax import lax
from jax.sharding import PartitionSpec as P

C = 32768
ITERS = 2


decay_rate = 0.95
linear_coef = 3.4445
square_coef = -4.775
quint_coef = 2.0315
epsilon = 1e-07


def gram_total(iterate):
    local_gram = lax.dot_general(
        iterate, iterate, (((1,), (1,)), ((), ())), precision=lax.Precision.HIGHEST
    )
    return lax.psum(local_gram, ("dp", "head"))


def local(latents, targets, kv_weight, momentum):
    latent_width = momentum.shape[0]
    sub_width = momentum.shape[2]
    total_tokens = latents.shape[0] * lax.axis_size("dp")
    residual = (
        jnp.dot(latents, kv_weight, preferred_element_type=jnp.float32)
        - targets.astype(jnp.float32)
    ).astype(jnp.bfloat16)
    gradient = lax.psum_scatter(
        lax.dot_general(
            residual, latents, (((0,), (0,)), ((), ())), preferred_element_type=jnp.float32
        ),
        "dp",
        scatter_dimension=0,
        tiled=True,
    ).T
    gradient = gradient * (1.0 / math.sqrt(total_tokens))
    previous = momentum.reshape(latent_width, sub_width)
    momentum_new = decay_rate * previous + gradient
    nesterov = gradient + decay_rate * momentum_new
    squares = lax.psum(jnp.sum(nesterov * nesterov), ("dp", "head"))
    inverse = 1.0 / (jnp.sqrt(squares) + epsilon)
    iterate = nesterov * inverse
    gram_matrix = gram_total(iterate)
    for iteration in range(ITERS):
        if iteration > 0:
            gram_matrix = gram_total(iterate)
        polynomial = square_coef * gram_matrix + quint_coef * jnp.dot(
            gram_matrix, gram_matrix, precision=lax.Precision.HIGHEST
        )
        iterate = linear_coef * iterate + jnp.dot(
            polynomial, iterate, precision=lax.Precision.HIGHEST
        )
    update = iterate * math.sqrt(C)
    return (
        momentum_new.reshape(latent_width, 1, sub_width),
        update.reshape(latent_width, 1, sub_width),
    )


def solution(mesh):
    return jax.shard_map(
        local,
        mesh=mesh,
        in_specs=(P("dp", None), P("dp", "head"), P(None, "head"), P(None, "head", "dp")),
        out_specs=(P(None, "head", "dp"), P(None, "head", "dp")),
        check_vma=False,
    )
```

profile of v0, /device:TPU:1, one launch (start us, length us, event | category | flops | bytes accessed | tf_op | source)
XLA Modules:
  0.0 706.3 jit_solution(13692104984853528014)
XLA Ops:
  7.2 0.0 copy-start
  7.2 0.0 reduce-scatter.2.cloned.1.call-start
  7.2 1.5 copy-done
  8.8 4.0 fusion.3
  12.8 0.0 reduce-scatter.2.cloned.1.call-update
  12.8 0.0 all-reduce.3.cloned.1.call-start
  12.9 0.9 copy-done.2
  13.7 0.1 copy.6
  13.9 83.9 %reduce-scatter.2.cloned.1.call-done = f32[128,512]{1,0:T(8,128)} async-done(((f32[2048,512]{1,0:T(8,128)}), f32[128,512]{1,0:T(8,128)}) %reduce-scatter.2.cloned.1.call-update) | async-done | bytes 262160 | tf_op jit(solution)/shard_map/reduce_scatter | solution.py:34
  97.8 1.6 multiply_reduce_fusion
  99.4 77.2 %psum.21 = f32[]{:T(128)} all-reduce(f32[]{:T(128)} %get-tuple-element.4), channel_id=1, replica_groups=mesh['dp'=16,'head'=16] {'dp','head'}, use_global_device_ids=true, to_apply=%region_2.0 | all-reduce | flops 1 | bytes 8 | tf_op jit(solution)/shard_map/psum | solution.py:46
  177.3 3.1 fusion.7
  180.5 0.0 all-reduce.3.cloned.1.call-update
  180.5 0.0 all-reduce.5.cloned.1.call-start
  180.5 251.3 %all-reduce.3.cloned.1.call-done = f32[512,512]{1,0:T(8,128)} async-done(((f32[512,512]{1,0:T(8,128)}), f32[512,512]{1,0:T(8,128)}) %all-reduce.3.cloned.1.call-update) | async-done | bytes 1048592 | tf_op jit(solution)/shard_map/psum | solution.py:23
  431.8 3.9 fusion.2
  435.8 1.2 convolution_add_fusion.1
  437.0 2.1 fusion.13
  439.1 0.0 all-reduce.5.cloned.1.call-update
  439.1 0.8 copy.9
  439.9 253.9 %all-reduce.5.cloned.1.call-done = f32[512,512]{1,0:T(8,128)} async-done(((f32[512,512]{1,0:T(8,128)}), f32[512,512]{1,0:T(8,128)}) %all-reduce.5.cloned.1.call-update) | async-done | bytes 1048592 | tf_op jit(solution)/shard_map/psum | solution.py:23
  693.8 3.9 fusion.1
  697.7 1.2 fusion.5
  698.9 0.8 copy.10
  (3 shorter events, 0.0 us)
Async XLA Ops:
  7.2 1.6 copy-start
  7.2 90.6 %reduce-scatter.2.cloned.1.call-start = ((), (), s32[]{:S(2)}) async-start(), calls=%async_computation.1 | async-start | bytes 4456448 | tf_op jit(solution)/shard_map/reduce_scatter | solution.py:34
  12.8 0.9 copy-start.2
  12.8 419.0 %all-reduce.3.cloned.1.call-start = ((), (), s32[]{:S(2)}) async-start(), calls=%async_computation.2 | async-start | bytes 2097152 | tf_op jit(solution)/shard_map/psum | solution.py:23
  180.5 255.3 %copy-start.1 = (f32[128,512]{1,0:T(8,128)S(1)}, f32[128,512]{1,0:T(8,128)}, u32[]{:S(2)}) copy-start(f32[128,512]{1,0:T(8,128)} %reduce-scatter.2.cloned.1.call-done) | copy-start | bytes 786436
  180.5 513.3 %all-reduce.5.cloned.1.call-start = ((), (), s32[]{:S(2)}) async-start(), calls=%async_computation.3 | async-start | bytes 2097152 | tf_op jit(solution)/shard_map/psum | solution.py:23
Sparse Core Ops, SparseCore 0:
  12.9 84.8 reduce-scatter.1
  180.6 251.1 all-reduce.2
  439.2 254.5 all-reduce.4
where the time goes:
time: 707 us; the launch traced here: 706 us
  waiting for transfers between devices  589 us (83%)
  blocking collectives  77.2 us (11%)
  matrix products  19.5 us (3%)
  between operations  14.5 us (2%)
    psum x2, waiting for transfers between devices, gram_total(): return lax.psum(local_gram, ('dp', 'head'))  505 us
    reduce_scatter x1, waiting for transfers between devices, local(): lax.psum_scatter(lax.dot_general(residual, latents, (((0,), (0,)), ((), (...  83.9 us
    psum x1, blocking collectives, local(): squares = lax.psum(jnp.sum(nesterov * nesterov), ('dp', 'head'))  77.2 us
  transfers between devices with their start and end apart: 3, of which 3 were waited for; matrix products, arithmetic and copies ran while one was open for 0% of the time, Pallas kernels for 0%

commit v1 on v0

v1 whole, which is shorter than its diff:
```python
import math

import jax
import jax.numpy as jnp
from jax import lax
from jax.sharding import PartitionSpec as P

C = 32768

decay_rate = 0.95
linear_coef = 3.4445
square_coef = -4.775
quint_coef = 2.0315
epsilon = 1e-07
HIGHEST = lax.Precision.HIGHEST


def local(latents, targets, kv_weight, momentum):
    latent_width = momentum.shape[0]
    sub_width = momentum.shape[2]
    total_tokens = latents.shape[0] * lax.axis_size("dp")
    all_latents = lax.all_gather(latents, "dp", axis=0, tiled=True)
    my_targets = lax.all_to_all(targets, "dp", split_axis=1, concat_axis=0, tiled=True)
    start = lax.axis_index("dp") * sub_width
    my_weight = lax.dynamic_slice(kv_weight, (0, start), (latent_width, sub_width))
    residual = (
        jnp.dot(all_latents, my_weight, preferred_element_type=jnp.float32)
        - my_targets.astype(jnp.float32)
    ).astype(jnp.bfloat16)
    gradient = lax.dot_general(
        all_latents, residual, (((0,), (0,)), ((), ())), preferred_element_type=jnp.float32
    ) * (1.0 / math.sqrt(total_tokens))
    momentum_new = decay_rate * momentum.reshape(latent_width, sub_width) + gradient
    nesterov = gradient + decay_rate * momentum_new
    gram = lax.psum(
        lax.dot_general(nesterov, nesterov, (((1,), (1,)), ((), ())), precision=HIGHEST),
        ("dp", "head"),
    )
    inverse = 1.0 / (jnp.sqrt(jnp.trace(gram)) + epsilon)
    gram = gram * (inverse * inverse)
    eye = jnp.eye(latent_width, dtype=jnp.float32)
    first = linear_coef * eye + square_coef * gram + quint_coef * jnp.dot(gram, gram, precision=HIGHEST)
    second_gram = jnp.dot(first, jnp.dot(gram, first, precision=HIGHEST), precision=HIGHEST)
    second = (
        linear_coef * eye
        + square_coef * second_gram
        + quint_coef * jnp.dot(second_gram, second_gram, precision=HIGHEST)
    )
    iterate = jnp.dot(first, nesterov * (inverse * math.sqrt(C)), precision=HIGHEST)
    update = jnp.dot(second, iterate, precision=HIGHEST)
    return (
        momentum_new.reshape(latent_width, 1, sub_width),
        update.reshape(latent_width, 1, sub_width),
    )


def solution(mesh):
    return jax.shard_map(
        local,
        mesh=mesh,
        in_specs=(P("dp", None), P("dp", "head"), P(None, "head"), P(None, "head", "dp")),
        out_specs=(P(None, "head", "dp"), P(None, "head", "dp")),
        check_vma=False,
    )
```

time: 707 us -> 347 us (0.49)
  waiting for transfers between devices: 589 us -> 295 us
  blocking collectives: 77.2 us -> 0 us
  starting transfers between devices: 0.12 us -> 7.71 us
    psum x2 -> x1, waiting for transfers between devices: 505 us -> 254 us  [local(): lax.psum(lax.dot_general(nesterov, nesterov, (((1,), (1,)), ((), ())), pr...]
    reduce_scatter x1 -> x0, waiting for transfers between devices: 83.9 us -> none  [local(): lax.psum_scatter(lax.dot_general(residual, latents, (((0,), (0,)), ((), (...]
    psum x1 -> x0, blocking collectives: 77.2 us -> none  [local(): squares = lax.psum(jnp.sum(nesterov * nesterov), ('dp', 'head'))]
    all_gather x0 -> x1, waiting for transfers between devices: none -> 30.4 us  [local(): all_latents = lax.all_gather(latents, 'dp', axis=0, tiled=True)]
    all_to_all x0 -> x1, waiting for transfers between devices: none -> 10.2 us  [local(): lax.all_to_all(targets, 'dp', split_axis=1, concat_axis=0, tiled=True)]
    all_to_all x0 -> x1, starting transfers between devices: none -> 7.64 us  [local(): lax.all_to_all(targets, 'dp', split_axis=1, concat_axis=0, tiled=True)]
    dot_general x7 -> x8, matrix products: 19.5 us -> 18.1 us  [the longest x1 4.05 us: local(): jnp.dot(gram, gram, precision=HIGHEST)]
  transfers between devices with their start and end apart: 3 -> 3, of which waited for: 3 -> 3; matrix products, arithmetic and copies ran while one was open for 0% -> 2% of each run, Pallas kernels for 0% -> 0%
where the time goes in v1:
time: 347 us; the launch traced here: 346 us
  waiting for transfers between devices  295 us (85%)
  matrix products  18.1 us (5%)
  between operations  14.9 us (4%)
  starting transfers between devices  7.71 us (2%)
  local copies, waits for them, and re-layouts  6.89 us (2%)
    psum x1, waiting for transfers between devices, local(): lax.psum(lax.dot_general(nesterov, nesterov, (((1,), (1,)), ((), ())), pr...  254 us
    all_gather x1, waiting for transfers between devices, local(): all_latents = lax.all_gather(latents, 'dp', axis=0, tiled=True)  30.4 us
    all_to_all x1, waiting for transfers between devices, local(): lax.all_to_all(targets, 'dp', split_axis=1, concat_axis=0, tiled=True)  10.2 us
    all_to_all x1, starting transfers between devices, local(): lax.all_to_all(targets, 'dp', split_axis=1, concat_axis=0, tiled=True)  7.64 us
  transfers between devices with their start and end apart: 3, of which 3 were waited for; matrix products, arithmetic and copies ran while one was open for 2% of the time, Pallas kernels for 0%

profile of v1, /device:TPU:1, one launch (start us, length us, event | category | flops | bytes accessed | tf_op | source)
XLA Modules:
  0.0 345.9 jit_solution(12459691134939242747)
XLA Ops:
  7.2 0.0 copy-start
  7.2 0.0 all-gather.2.cloned.1.call-start
  7.2 0.7 all-gather.2.cloned.1.call-update
  7.9 2.0 copy.13
  10.0 7.6 %all-to-all-start = ((bf16[128,16,128]{0,2,1:T(8,128)(2,1)}), bf16[128,16,128]{0,2,1:T(8,128)(2,1)}, u32[]{:S(2)}, u32[]{:S(2)}) async-start(bf16[128,16,128]{0,2,1:T(8,128)(2,1)} %bitcast.2), calls=%async_computation | async-start | bytes 1048576 | tf_op jit(solution)/shard_map/all_to_all | solution.py:23
  17.6 0.0 all-reduce.2.cloned.1.call-start
  17.7 0.1 copy.12
  17.8 10.2 %all-to-all-done = bf16[128,16,128]{0,2,1:T(8,128)(2,1)} async-done(((bf16[128,16,128]{0,2,1:T(8,128)(2,1)}), bf16[128,16,128]{0,2,1:T(8,128)(2,1)}, u32[]{:S(2)}, u32[]{:S(2)}) %all-to-all-start) | async-done | bytes 524320 | tf_op jit(solution)/shard_map/all_to_all | solution.py:23
  28.0 1.1 convert_bitcast_fusion
  29.1 1.3 copy.14
  30.4 2.5 copy.15
  33.0 30.4 %all-gather.2.cloned.1.call-done = bf16[2048,512]{1,0:T(8,128)(2,1)} async-done(((bf16[128,512]{1,0:T(8,128)(2,1)}), bf16[2048,512]{1,0:T(8,128)(2,1)}) %all-gather.2.cloned.1.call-update) | async-done | bytes 2097168 | tf_op jit(solution)/shard_map/all_gather | solution.py:22
  63.4 3.7 %fusion.6 = f32[512,128]{0,1:T(8,128)S(1)} fusion(bf16[2048,512]{1,0:T(8,128)(2,1)} %all-gather.2.cloned.1.call-done, f32[2048,128]{0,1:T(8,128)} %copy.15, bf16[512,2048]{1,0:T(8,128)(2,1)S(1)} %copy-done, s32[]{:T(128)S(6)} %select_n.8), kind=kOutput, calls=%fused_computation.11 | convolution fusion | flops 537460736 | bytes 5636100 | tf_op jit(solution)/shard_map/dot_general | solution.py:30
  67.1 2.1 fusion.18
  69.1 0.0 all-reduce.2.cloned.1.call-update
  69.2 0.8 copy.16
  70.1 254.0 %all-reduce.2.cloned.1.call-done = f32[512,512]{1,0:T(8,128)} async-done(((f32[512,512]{1,0:T(8,128)}), f32[512,512]{1,0:T(8,128)}) %all-reduce.2.cloned.1.call-update) | async-done | bytes 1048592 | tf_op jit(solution)/shard_map/psum | solution.py:35
  324.1 1.9 select_reduce_fusion
  326.7 4.1 %fusion.3 = f32[512,512]{1,0:T(8,128)S(1)} fusion(f32[512,512]{1,0:T(8,128)} %all-reduce.2.cloned.1.call-done, f32[]{:T(128)S(6)} %mul.65), kind=kOutput, calls=%fused_computation.8 | convolution fusion | flops 1612709888 | bytes 2097156 | tf_op jit(solution)/shard_map/dot_general | solution.py:42
  330.8 1.0 fusion.12
  331.8 1.9 fusion.8
  333.7 1.8 fusion.23
  335.5 1.9 fusion.2
  337.4 1.7 fusion.24
  (6 shorter events, 0.1 us)
Async XLA Ops:
  7.2 56.2 %copy-start = (bf16[512,2048]{1,0:T(8,128)(2,1)S(1)}, bf16[512,2048]{1,0:T(8,128)(2,1)}, u32[]{:S(2)}) copy-start(bf16[512,2048]{1,0:T(8,128)(2,1)} %param.6) | copy-start | bytes 6291460
  7.2 10.5 %copy-start.2 = (f32[512,1,128]{2,1,0:T(1,128)S(1)}, f32[512,1,128]{2,1,0:T(1,128)}, u32[]{:S(2)}) copy-start(f32[512,1,128]{2,1,0:T(1,128)} %param.7) | copy-start | bytes 786436
  7.2 56.2 %all-gather.2.cloned.1.call-start = ((), (), s32[]{:S(2)}) async-start(), calls=%async_computation.1 | async-start | bytes 2228224 | tf_op jit(solution)/shard_map/all_gather | solution.py:22
  10.0 18.0 %all-to-all-start = ((bf16[128,16,128]{0,2,1:T(8,128)(2,1)}), bf16[128,16,128]{0,2,1:T(8,128)(2,1)}, u32[]{:S(2)}, u32[]{:S(2)}) async-start(bf16[128,16,128]{0,2,1:T(8,128)(2,1)} %bitcast.2), calls=%async_computation | async-start | bytes 1048576 | tf_op jit(solution)/shard_map/all_to_all | solution.py:23
  17.6 306.4 %all-reduce.2.cloned.1.call-start = ((), (), s32[]{:S(2)}) async-start(), calls=%async_computation.2 | async-start | bytes 2097152 | tf_op jit(solution)/shard_map/psum | solution.py:35
  326.7 5.1 %copy-start.1 = (f32[512,512]{1,0:T(8,128)S(1)}, f32[512,512]{1,0:T(8,128)}, u32[]{:S(2)}) copy-start(f32[512,512]{1,0:T(8,128)} %all-reduce.2.cloned.1.call-done) | copy-start | bytes 3145732
Sparse Core Ops, SparseCore 0:
  10.5 52.8 all-gather.1
  69.3 254.7 all-reduce.1

commit v2 on v1

v2 whole, which is shorter than its diff:
```python
import functools
import math

import jax
import jax.numpy as jnp
from jax import lax
from jax.experimental import pallas as pl
from jax.experimental.pallas import tpu as pltpu
from jax.sharding import PartitionSpec as P

MESH = pl.DeviceIdType.MESH
F32, BF16 = jnp.float32, jnp.bfloat16

R = 512
C = 32768
TOKENS = 2048
NX = 4
NZ = 8
COLS = 128
HALF = 64
CHIPS = NX * NX
PIECE = 5 * 128 // CHIPS

decay_rate = 0.95
linear_coef = 3.4445
square_coef = -4.775
quint_coef = 2.0315
epsilon = 1e-07

OFFSETS = [(0, 1), (0, 3), (1, 0), (3, 0), (1, 1), (1, 3), (3, 1), (3, 3), (0, 2), (2, 0), (1, 2), (3, 2), (2, 1), (2, 3), (2, 2)]
RING = (1, 3, 2)
ZRING = (4, 3, 5, 2, 6, 1, 7)
BLOCKS = (((0, 0), (0, 1), (1, 1), (0, 2), (0, 3)), ((2, 2), (2, 3), (3, 3), (1, 2), (1, 3)))


def split(value):
    high = value.astype(BF16)
    return high, (value - high.astype(F32)).astype(BF16)


def dot(a, b):
    return jnp.dot(a, b, preferred_element_type=F32)


def dot_nt(a, b):
    return lax.dot_general(a, b, (((1,), (1,)), ((), ())), preferred_element_type=F32)


def dot_tn(a, b):
    return lax.dot_general(a, b, (((0,), (0,)), ((), ())), preferred_element_type=F32)


def multiply(a, b):
    (ah, al), (bh, bl) = a, b
    return dot(ah, bh) + (dot(ah, bl) + dot(al, bh))


def kernel(
    lat, tgt, wgt, mom, mom_out, upd_out,
    lbuf, tbuf, wbuf, mbuf, gown, gsib, xbuf, gs, rbuf, pz, zbuf, gf, gm, mh, ml, ph, pl_lo, qh, ql, pm,
    send_a, send_b, local_sem, sem_l, sem_t, sem_w, sem_m, sem_g, sem_r, sem_z, sem_f, sem_s,
):
    chip = lax.axis_index("dp")
    head = lax.axis_index("head")
    x, y = lax.div(chip, NX), lax.rem(chip, NX)
    z, c = lax.div(head, 2), lax.rem(head, 2)
    sibling = (chip, z * 2 + (1 - c))
    p1 = jnp.where(c == 0, y, x)
    p2 = jnp.where(c == 0, x, y)
    stride1 = jnp.where(c == 0, 1, NX)
    stride2 = jnp.where(c == 0, NX, 1)

    def step(p, by):
        return lax.rem(p + by, NX)

    def ring1(by):
        return (step(p1, by) * stride1 + p2 * stride2, head)

    def ring2(by):
        return (p1 * stride1 + step(p2, by) * stride2, head)

    def plane(offset):
        return step(x, offset[0]) * NX + step(y, offset[1])

    my_cols = pl.ds(pl.multiple_of(c * COLS, COLS), COLS)
    block_cols = pl.ds(pl.multiple_of(chip * COLS, COLS), COLS)
    my_slot = p2 * NX + p1

    def remote(src, dst, ssem, rsem, device):
        return pltpu.make_async_remote_copy(
            src_ref=src, dst_ref=dst, send_sem=ssem, recv_sem=rsem, device_id=device, device_id_type=MESH
        )

    local = [
        pltpu.make_async_copy(wgt.at[:, block_cols], wbuf.at[:, my_cols], local_sem.at[0]),
        pltpu.make_async_copy(lat.at[pl.ds(pl.multiple_of(c * HALF, HALF), HALF)], lbuf.at[my_slot], local_sem.at[1]),
        pltpu.make_async_copy(
            tgt.at[pl.ds(pl.multiple_of(c * HALF, HALF), HALF), block_cols], tbuf.at[my_slot, :, my_cols], local_sem.at[2]
        ),
        pltpu.make_async_copy(mom, mbuf.at[:, my_cols], local_sem.at[3]),
    ]
    for copy in local:
        copy.start()

    barrier = pltpu.get_barrier_semaphore()
    partners = 0
    for offset in OFFSETS:
        for core in range(2):
            pl.semaphore_signal(barrier, inc=1, device_id=(plane(offset), z * 2 + core), device_id_type=MESH)
            partners += 1
    for by in ZRING:
        pl.semaphore_signal(barrier, inc=1, device_id=(chip, lax.rem(z + by, NZ) * 2 + c), device_id_type=MESH)
        partners += 1
    pl.semaphore_signal(barrier, inc=1, device_id=sibling, device_id_type=MESH)
    pl.semaphore_wait(barrier, partners + 1)

    sends = []
    count_a = [0]

    def send_now(src, dst, rsem, device):
        copy = remote(src, dst, send_a.at[count_a[0]], rsem, device)
        count_a[0] += 1
        copy.start()
        sends.append(copy)

    my_half = lat.at[pl.ds(pl.multiple_of(c * HALF, HALF), HALF)]
    for by in RING:
        send_now(my_half, lbuf.at[my_slot], sem_l.at[my_slot], ring1(by))
    for by in RING:
        send_now(my_half, lbuf.at[my_slot], sem_l.at[my_slot], ring2(by))
    slot_on = (x * NX + y, y * NX + x)
    for offset in OFFSETS:
        to = plane(offset)
        to_cols = pl.ds(pl.multiple_of(to * COLS, COLS), COLS)
        for core in range(2):
            send_now(
                tgt.at[pl.ds(core * HALF, HALF), to_cols],
                tbuf.at[slot_on[core], :, my_cols],
                sem_t.at[slot_on[core]],
                (to, z * 2 + core),
            )
    sib_slot = p1 * NX + p2
    send_now(wgt.at[:, block_cols], wbuf.at[:, my_cols], sem_w, sibling)
    send_now(
        tgt.at[pl.ds(pl.multiple_of((1 - c) * HALF, HALF), HALF), block_cols],
        tbuf.at[sib_slot, :, my_cols],
        sem_t.at[sib_slot],
        sibling,
    )
    send_now(mom, mbuf.at[:, my_cols], sem_m, sibling)

    def wait_recv(ref, sem):
        remote(ref, ref, send_a.at[0], sem, sibling).wait_recv()

    for by in RING:
        slot = p2 * NX + step(p1, by)
        wait_recv(lbuf.at[slot], sem_l.at[slot])
        for by2 in RING:
            send_now(lbuf.at[slot], lbuf.at[slot], sem_l.at[slot], ring2(by2))

    sib_cols = pl.ds(pl.multiple_of((1 - c) * COLS, COLS), COLS)
    for copy in local:
        copy.wait()
    wait_recv(wbuf.at[:, sib_cols], sem_w)
    weight = wbuf[...]

    for group, by in enumerate((0,) + RING):
        q2 = step(p2, by)
        for by1 in (0,) + RING:
            slot = q2 * NX + step(p1, by1)
            if by == 0 and by1 == 0:
                wait_recv(tbuf.at[slot, :, sib_cols], sem_t.at[slot])
            else:
                wait_recv(tbuf.at[slot], sem_t.at[slot])
            if by != 0:
                wait_recv(lbuf.at[slot], sem_l.at[slot])
        tokens = NX * HALF
        latent = lbuf[pl.ds(q2 * NX, NX)].reshape(tokens, R)
        target = tbuf[pl.ds(q2 * NX, NX)].reshape(tokens, 2 * COLS)
        residual = (dot(latent, weight) - target.astype(F32)).astype(BF16)
        part = dot_tn(latent, residual)
        if group == 0:
            gown[...] = part
        else:
            gown[...] += part

    exchange = remote(gown, gsib, send_b.at[0], sem_g, sibling)
    exchange.start()
    wait_recv(mbuf.at[:, sib_cols], sem_m)
    exchange.wait_recv()
    gradient = (gown[...] + gsib[...]) * (1.0 / math.sqrt(TOKENS))
    momentum_new = decay_rate * mbuf[...] + gradient
    nesterov = gradient + decay_rate * momentum_new
    mbuf[...] = momentum_new
    gsib[...] = nesterov
    xbuf[0], xbuf[1] = split(nesterov)
    mom_out[...] = mbuf[:, my_cols]

    def rows(start, size):
        at = pl.ds(pl.multiple_of(start, 128), size)
        return xbuf[0, at, :], xbuf[1, at, :]

    def gram(a, b):
        (ah, al), (bh, bl) = a, b
        return dot_nt(ah, bh) + (dot_nt(ah, bl) + dot_nt(al, bh))

    square = rows(c * 256, 256)
    diagonal = gram(square, square)
    gs[0:128, :] = diagonal[:128, :128]
    gs[128:256, :] = diagonal[:128, 128:]
    gs[256:384, :] = diagonal[128:, 128:]
    upper = gram(rows(c * 128, 128), rows(256, 256))
    gs[384:512, :] = upper[:, :128]
    gs[512:640, :] = upper[:, 128:]

    def piece(of):
        return pl.ds(pl.multiple_of(of * PIECE, 8), PIECE)

    count_b = [1]

    def send_b_now(src, dst, rsem, device):
        copy = remote(src, dst, send_b.at[count_b[0]], rsem, device)
        count_b[0] += 1
        copy.start()
        sends.append(copy)

    for k, offset in reversed(list(enumerate(OFFSETS))):
        to = plane(offset)
        send_b_now(gs.at[piece(to)], rbuf.at[k], sem_r, (to, head))
    wait_recv(rbuf, sem_r)
    total = gs[piece(chip), :]
    for k in range(CHIPS - 1):
        total = total + rbuf[k]
    pz[...] = total
    for by in ZRING:
        send_b_now(pz, zbuf.at[by - 1], sem_z, (chip, lax.rem(z + by, NZ) * 2 + c))
    wait_recv(zbuf, sem_z)
    for k in range(NZ - 1):
        total = total + zbuf[k]
    gf[c, piece(chip), :] = total
    for k, offset in reversed(list(enumerate(OFFSETS))):
        send_b_now(gf.at[c, piece(chip)], gf.at[c, piece(chip)], sem_f.at[k], (plane(offset), head))
    send_b_now(gf.at[c, piece(chip)], gf.at[c, piece(chip)], sem_s, sibling)
    for k, offset in enumerate(OFFSETS):
        source = plane(((4 - offset[0]) % 4, (4 - offset[1]) % 4))
        wait_recv(gf.at[c, piece(source)], sem_f.at[k])
        send_b_now(gf.at[c, piece(source)], gf.at[c, piece(source)], sem_s, sibling)
    wait_recv(gf.at[1 - c], sem_s)

    line = lax.broadcasted_iota(jnp.int32, (128, 128), 0)
    column = lax.broadcasted_iota(jnp.int32, (128, 128), 1)
    diag = line == column
    trace = jnp.zeros((1, 1), F32)
    for half in range(2):
        both = gf[half, 0:128, :] + gf[half, 256:384, :]
        trace = trace + jnp.sum(jnp.where(diag, both, 0.0), keepdims=True)
    inverse = 1.0 / (jnp.sqrt(trace) + epsilon)
    inverse2 = inverse * inverse
    for half in range(2):
        for index, (i, j) in enumerate(BLOCKS[half]):
            block = gf[half, index * 128 : (index + 1) * 128, :] * inverse2
            gm[i * 128 : (i + 1) * 128, j * 128 : (j + 1) * 128] = block
            if i != j:
                gm[j * 128 : (j + 1) * 128, i * 128 : (i + 1) * 128] = block.T
    eye_line = lax.broadcasted_iota(jnp.int32, (R, R), 0)
    eye_column = lax.broadcasted_iota(jnp.int32, (R, R), 1)
    identity = jnp.where(eye_line == eye_column, linear_coef, 0.0).astype(F32)

    mh[...], ml[...] = split(gm[...])
    first = identity + square_coef * gm[...] + quint_coef * multiply((mh[...], ml[...]), (mh[...], ml[...]))
    ph[...], pl_lo[...] = split(first)
    iterate = gsib[:, my_cols] * (inverse * math.sqrt(C))
    iterate = multiply((ph[...], pl_lo[...]), split(iterate))
    qh[...], ql[...] = split(multiply((ph[...], pl_lo[...]), (mh[...], ml[...])))
    pm[...] = multiply((qh[...], ql[...]), (ph[...], pl_lo[...]))
    mh[...], ml[...] = split(pm[...])
    second = identity + square_coef * pm[...] + quint_coef * multiply((mh[...], ml[...]), (mh[...], ml[...]))
    ph[...], pl_lo[...] = split(second)
    upd_out[...] = multiply((ph[...], pl_lo[...]), split(iterate))

    for copy in sends:
        copy.wait_send()
    exchange.wait_send()


def local(latents, targets, kv_weight, momentum):
    previous = momentum.reshape(R, COLS)
    dma = pltpu.SemaphoreType.DMA
    any_space = pl.BlockSpec(memory_space=pl.ANY)
    vmem = pl.BlockSpec(memory_space=pltpu.VMEM)
    momentum_new, update = pl.pallas_call(
        kernel,
        out_shape=(jax.ShapeDtypeStruct((R, COLS), F32), jax.ShapeDtypeStruct((R, COLS), F32)),
        in_specs=[any_space] * 4,
        out_specs=(vmem, vmem),
        scratch_shapes=[
            pltpu.VMEM((CHIPS, HALF, R), BF16),
            pltpu.VMEM((CHIPS, HALF, 2 * COLS), BF16),
            pltpu.VMEM((R, 2 * COLS), BF16),
            pltpu.VMEM((R, 2 * COLS), F32),
            pltpu.VMEM((R, 2 * COLS), F32),
            pltpu.VMEM((R, 2 * COLS), F32),
            pltpu.VMEM((2, R, 2 * COLS), BF16),
            pltpu.VMEM((5 * 128, 128), F32),
            pltpu.VMEM((CHIPS - 1, PIECE, 128), F32),
            pltpu.VMEM((PIECE, 128), F32),
            pltpu.VMEM((NZ - 1, PIECE, 128), F32),
            pltpu.VMEM((2, 5 * 128, 128), F32),
            pltpu.VMEM((R, R), F32),
            pltpu.VMEM((R, R), BF16),
            pltpu.VMEM((R, R), BF16),
            pltpu.VMEM((R, R), BF16),
            pltpu.VMEM((R, R), BF16),
            pltpu.VMEM((R, R), BF16),
            pltpu.VMEM((R, R), BF16),
            pltpu.VMEM((R, R), F32),
            dma((48,)),
            dma((56,)),
            dma((4,)),
            dma((CHIPS,)),
            dma((CHIPS,)),
            dma,
            dma,
            dma,
            dma,
            dma,
            dma((CHIPS - 1,)),
            dma,
        ],
        compiler_params=pltpu.CompilerParams(
            collective_id=0, has_side_effects=True, vmem_limit_bytes=56 << 20
        ),
        name="muon_step",
    )(latents, targets, kv_weight, previous)
    return momentum_new.reshape(R, 1, COLS), update.reshape(R, 1, COLS)


def solution(mesh):
    return jax.shard_map(
        local,
        mesh=mesh,
        in_specs=(P("dp", None), P("dp", "head"), P(None, "head"), P(None, "head", "dp")),
        out_specs=(P(None, "head", "dp"), P(None, "head", "dp")),
        check_vma=False,
    )
```

time: 347 us -> 61.5 us (0.18)
  waiting for transfers between devices: 295 us -> 0 us
  Pallas kernels: 0 us -> 57.4 us
  matrix products: 18.1 us -> 0 us
  between operations: 14.9 us -> 0.64 us
  starting transfers between devices: 7.71 us -> 0 us
  local copies, waits for them, and re-layouts: 6.89 us -> 3.34 us
    psum x1 -> x0, waiting for transfers between devices: 254 us -> none  [local(): lax.psum(lax.dot_general(nesterov, nesterov, (((1,), (1,)), ((), ())), pr...]
    pallas_call x0 -> x1, Pallas kernels: none -> 57.4 us  [local(): pl.pallas_call(kernel, out_shape=(jax.ShapeDtypeStruct((R, COLS), F32), j...]
    all_gather x1 -> x0, waiting for transfers between devices: 30.4 us -> none  [local(): all_latents = lax.all_gather(latents, 'dp', axis=0, tiled=True)]
    dot_general x8 -> x0, matrix products: 18.1 us -> none  [the longest x1 4.05 us: local(): jnp.dot(gram, gram, precision=HIGHEST)]
    all_to_all x1 -> x0, waiting for transfers between devices: 10.2 us -> none  [local(): lax.all_to_all(targets, 'dp', split_axis=1, concat_axis=0, tiled=True)]
    all_to_all x1 -> x0, starting transfers between devices: 7.64 us -> none  [local(): lax.all_to_all(targets, 'dp', split_axis=1, concat_axis=0, tiled=True)]
    convert_element_type x2 -> x0, local copies, waits for them, and re-layouts: 3.86 us -> none  [local(): my_targets.astype(jnp.float32)]
  transfers between devices with their start and end apart: 3 -> 0, of which waited for: 3 -> 0; matrix products, arithmetic and copies ran while one was open for 2% -> 0% of each run, Pallas kernels for 0% -> 0%
where the time goes in v2:
time: 61.5 us; the launch traced here: 61.4 us
  Pallas kernels  57.4 us (93%)
  local copies, waits for them, and re-layouts  3.34 us (5%)
  between operations  0.64 us (1%)
    pallas_call x1, Pallas kernels, local(): pl.pallas_call(kernel, out_shape=(jax.ShapeDtypeStruct((R, COLS), F32), j...  57.4 us
    unnamed x2, local copies, waits for them, and re-layouts  3.34 us

profile of v2, /device:TPU:1, one launch (start us, length us, event | category | flops | bytes accessed | tf_op | source)
XLA Modules:
  0.0 61.4 jit_solution(15375386284620096353)
XLA Ops:
  0.6 57.4 %muon_step.1 = (f32[512,128]{1,0:T(8,128)}, f32[512,128]{1,0:T(8,128)}) custom-call(bf16[128,512]{1,0:T(8,128)(2,1)} %lat.1, bf16[128,2048]{1,0:T(8,128)(2,1)} %tgt.1, bf16[512,2048]{1,0:T(8,128)(2,1)} %wgt.1, f32[512,128]{1,0:T(8,128)} %bitcast.7), custom_call_target="tpu_custom_call" | custom-call | tf_op jit(solution)/shard_map/muon_step/pallas_call | solution.py:291
  58.0 1.7 %copy.10 = f32[512,1,128]{2,1,0:T(1,128)} copy(f32[512,1,128]{2,1,0:T(1,128)} %bitcast.9) | data formatting | bytes 524288
  59.7 1.7 %copy.11 = f32[512,1,128]{2,1,0:T(1,128)} copy(f32[512,1,128]{2,1,0:T(1,128)} %bitcast.8) | data formatting | bytes 524288

commit v3 on v2

v3 whole, which is shorter than its diff:
```python
import math

import jax
import jax.numpy as jnp
from jax import lax
from jax.experimental import pallas as pl
from jax.experimental.pallas import tpu as pltpu
from jax.sharding import PartitionSpec as P

MESH = pl.DeviceIdType.MESH
F32, BF16 = jnp.float32, jnp.bfloat16

R = 512
C = 32768
TOKENS = 2048
NX = 4
NZ = 8
COLS = 128
HALF = 64
QUARTER = 32
CHIPS = NX * NX
PIECE = 5 * 128 // CHIPS
CHUNK = 256

decay_rate = 0.95
linear_coef = 3.4445
square_coef = -4.775
quint_coef = 2.0315
epsilon = 1e-07

OFFSETS = [(0, 1), (0, 3), (1, 0), (3, 0), (1, 1), (1, 3), (3, 1), (3, 3), (0, 2), (2, 0), (1, 2), (3, 2), (2, 1), (2, 3), (2, 2)]
FAR_FIRST = list(reversed(list(enumerate(OFFSETS))))
RING = (1, 3, 2)
ZRING = (4, 3, 5, 2, 6, 1, 7)
BLOCKS = (((0, 0), (256, 256)), ((0, 128), (256, 256)), ((128, 128), (256, 256)), ((0, 256), (128, 0)), ((0, 384), (128, 0)))


def split(value):
    high = value.astype(BF16)
    return high, (value - high.astype(F32)).astype(BF16)


def dot(a, b):
    return jnp.dot(a, b, preferred_element_type=F32)


def dot_nt(a, b):
    return lax.dot_general(a, b, (((1,), (1,)), ((), ())), preferred_element_type=F32)


def dot_tn(a, b):
    return lax.dot_general(a, b, (((0,), (0,)), ((), ())), preferred_element_type=F32)


def kernel(
    lat, tgt, wgt, mom, mom_out, upd_out,
    lbuf, tstage, tbuf, wbuf, mbuf, gown, gsib, xbuf, nest, gs, rbuf, pz, zbuf, gf, gm, gh, gl, ph, plo,
    send_a, send_b, local_sem, sem_l, sem_lz, sem_t, sem_w, sem_m, sem_g, sem_r, sem_z, sem_f, sem_s, out_sem, ready,
):
    chip = lax.axis_index("dp")
    head = lax.axis_index("head")
    x, y = lax.div(chip, NX), lax.rem(chip, NX)
    z, c = lax.div(head, 2), lax.rem(head, 2)
    sibling = (chip, z * 2 + (1 - c))

    def step(p, by):
        return lax.rem(p + by, NX)

    def along_z(by):
        return (chip, lax.rem(z + by, NZ) * 2 + c)

    def plane(offset):
        return step(x, offset[0]) * NX + step(y, offset[1])

    def remote(src, dst, ssem, rsem, device):
        return pltpu.make_async_remote_copy(
            src_ref=src, dst_ref=dst, send_sem=ssem, recv_sem=rsem, device_id=device, device_id_type=MESH
        )

    def wait_recv(ref, sem):
        remote(ref, ref, send_a.at[0], sem, sibling).wait_recv()

    barrier = pltpu.get_barrier_semaphore()
    partners = 1
    for by in ZRING:
        pl.semaphore_signal(barrier, inc=1, device_id=along_z(by), device_id_type=MESH)
        partners += 1
    for _, offset in FAR_FIRST:
        pl.semaphore_signal(barrier, inc=1, device_id=(plane(offset), head), device_id_type=MESH)
        partners += 1
    pl.semaphore_signal(barrier, inc=1, device_id=sibling, device_id_type=MESH)

    zp = lax.rem(z, 2)
    block_cols = pl.ds(pl.multiple_of(chip * COLS, COLS), COLS)

    def quarter(of):
        return lat.at[pl.ds(pl.multiple_of(c * HALF + of * QUARTER, QUARTER), QUARTER)]

    for to in range(CHIPS):
        pltpu.make_async_copy(tgt.at[:, to * COLS : (to + 1) * COLS], tstage.at[to], local_sem.at[0]).start()
    own_weight = pltpu.make_async_copy(wgt.at[:, block_cols], wbuf.at[0], local_sem.at[1])
    own_weight.start()
    own_quarter = pltpu.make_async_copy(quarter(zp), lbuf.at[chip, zp], local_sem.at[2])
    own_quarter.start()
    pltpu.make_async_copy(quarter(1 - zp), lbuf.at[chip, 1 - zp], sem_lz.at[x]).start()
    own_momentum = pltpu.make_async_copy(mom, mbuf.at[0], local_sem.at[3])
    own_momentum.start()
    pl.semaphore_wait(barrier, partners)
    pl.semaphore_signal(ready, inc=1, device_id=sibling, device_id_type=MESH)

    sends = []
    count_a = [0]

    def send_now(src, dst, rsem, device):
        copy = remote(src, dst, send_a.at[count_a[0]], rsem, device)
        count_a[0] += 1
        copy.start()
        sends.append(copy)

    for _, offset in FAR_FIRST:
        send_now(quarter(zp), lbuf.at[chip, zp], sem_l.at[chip], (plane(offset), head))

    pltpu.make_async_copy(tstage, tstage, local_sem.at[0]).wait()
    my_rows = pl.ds(pl.multiple_of(c * HALF, HALF), HALF)
    sib_rows = pl.ds(pl.multiple_of((1 - c) * HALF, HALF), HALF)
    for _, offset in FAR_FIRST:
        to = plane(offset)
        send_now(tstage.at[to, my_rows], tbuf.at[0, chip], sem_t.at[x], (to, head))
    pl.semaphore_wait(ready, 1)
    for _, offset in FAR_FIRST:
        to = plane(offset)
        send_now(tstage.at[to, sib_rows], tbuf.at[1, chip], sem_t.at[x], (to, z * 2 + (1 - c)))
    own_weight.wait()
    send_now(wbuf.at[0], wbuf.at[1], sem_w, sibling)
    send_now(tstage.at[chip, sib_rows], tbuf.at[1, chip], sem_t.at[x], sibling)
    send_now(mom, mbuf.at[1], sem_m, sibling)
    pltpu.make_async_copy(tstage.at[chip, my_rows], tbuf.at[0, chip], sem_t.at[x]).start()

    flip = [0]

    def swap(slot):
        side = 1 if flip[0] % 2 == 0 else NZ - 1
        flip[0] += 1
        send_now(lbuf.at[slot, zp], lbuf.at[slot, zp], sem_lz.at[lax.div(slot, NX)], along_z(side))

    for offset in OFFSETS:
        slot = plane(offset)
        wait_recv(lbuf.at[slot, zp], sem_l.at[slot])
        swap(slot)

    own_quarter.wait()
    wait_recv(wbuf.at[1], sem_w)
    tokens = NX * HALF

    def group_of(by):
        return pl.ds(step(x, by) * NX, NX)

    def residual_of(by):
        group = group_of(by)
        wait_recv(tbuf.at[:, group], sem_t.at[step(x, by)])
        wait_recv(lbuf.at[group, 1 - zp], sem_lz.at[step(x, by)])
        weight = jnp.concatenate([wbuf[0], wbuf[1]], axis=1)
        target = jnp.concatenate([tbuf[0, group].reshape(tokens, COLS), tbuf[1, group].reshape(tokens, COLS)], axis=1)
        return (dot(lbuf[group].reshape(tokens, R), weight) - target.astype(F32)).astype(BF16)

    def add_gradient(by, residual, first):
        latent = lbuf[group_of(by)].reshape(tokens, R)
        part = dot_tn(latent, residual)
        for r in range(2):
            value = part[:, r * COLS : (r + 1) * COLS]
            if first:
                gown[r] = value
            else:
                gown[r] += value

    add_gradient(0, residual_of(0), True)
    add_gradient(1, residual_of(1), False)
    add_gradient(3, residual_of(3), False)

    residual = residual_of(2)
    for chunk in range(R // CHUNK):
        at = slice(chunk * CHUNK, (chunk + 1) * CHUNK)
        part = dot_tn(lbuf[group_of(2), :, :, at].reshape(tokens, CHUNK), residual)
        for r in range(2):
            gown[r, at, :] += part[:, r * COLS : (r + 1) * COLS]
            send_now(gown.at[r, at], gsib.at[1 - r, at], sem_g.at[chunk, r], sibling)
    wait_recv(mbuf.at[1], sem_m)
    own_momentum.wait()
    for chunk in range(R // CHUNK):
        at = slice(chunk * CHUNK, (chunk + 1) * CHUNK)
        for r in range(2):
            wait_recv(gsib.at[r, at], sem_g.at[chunk, 1 - r])
            gradient = (gown[r, at, :] + gsib[r, at, :]) * (1.0 / math.sqrt(TOKENS))
            momentum_new = decay_rate * mbuf[r, at, :] + gradient
            nesterov = gradient + decay_rate * momentum_new
            if r == 0:
                mbuf[0, at, :] = momentum_new
                nest[at, :] = nesterov
            xbuf[0, at, r * COLS : (r + 1) * COLS], xbuf[1, at, r * COLS : (r + 1) * COLS] = split(nesterov)
    momentum_done = pltpu.make_async_copy(mbuf.at[0], mom_out, out_sem)
    momentum_done.start()

    def rows(start, size):
        at = pl.ds(pl.multiple_of(start, 128), size)
        return xbuf[0, at, :], xbuf[1, at, :]

    def gram(a, b):
        (ah, al), (bh, bl) = a, b
        return dot_nt(ah, bh) + (dot_nt(ah, bl) + dot_nt(al, bh))

    square = rows(c * 256, 256)
    diagonal = gram(square, square)
    gs[0:128, :] = diagonal[:128, :128]
    gs[128:256, :] = diagonal[:128, 128:]
    gs[256:384, :] = diagonal[128:, 128:]
    upper = gram(rows(c * 128, 128), rows(256, 256))
    gs[384:512, :] = upper[:, :128]
    gs[512:640, :] = upper[:, 128:]

    def piece(of):
        return pl.ds(pl.multiple_of(of * PIECE, 8), PIECE)

    count_b = [0]

    def send_b_now(src, dst, rsem, device):
        copy = remote(src, dst, send_b.at[count_b[0]], rsem, device)
        count_b[0] += 1
        copy.start()
        sends.append(copy)

    for k, offset in FAR_FIRST:
        to = plane(offset)
        send_b_now(gs.at[piece(to)], rbuf.at[k], sem_r, (to, head))
    wait_recv(rbuf, sem_r)
    total = gs[piece(chip), :]
    for k in range(CHIPS - 1):
        total = total + rbuf[k]
    pz[...] = total
    for by in ZRING:
        send_b_now(pz, zbuf.at[by - 1], sem_z, along_z(by))
    wait_recv(zbuf, sem_z)
    for k in range(NZ - 1):
        total = total + zbuf[k]
    gf[c, piece(chip), :] = total
    for k, offset in FAR_FIRST:
        send_b_now(gf.at[c, piece(chip)], gf.at[c, piece(chip)], sem_f.at[k], (plane(offset), head))
    send_b_now(gf.at[c, piece(chip)], gf.at[c, piece(chip)], sem_s, sibling)
    for k, offset in enumerate(OFFSETS):
        source = plane(((4 - offset[0]) % 4, (4 - offset[1]) % 4))
        wait_recv(gf.at[c, piece(source)], sem_f.at[k])
        send_b_now(gf.at[c, piece(source)], gf.at[c, piece(source)], sem_s, sibling)

    def place(half):
        for index, (base, more) in enumerate(BLOCKS):
            line = pl.ds(pl.multiple_of(base[0] + half * more[0], 128), 128)
            column = pl.ds(pl.multiple_of(base[1] + half * more[1], 128), 128)
            block = gf[half, index * 128 : (index + 1) * 128, :]
            gm[line, column] = block
            gh[line, column], gl[line, column] = split(block)
            if index not in (0, 2):
                block = block.T
                gm[column, line] = block
                gh[column, line], gl[column, line] = split(block)

    place(c)
    wait_recv(gf.at[1 - c], sem_s)
    place(1 - c)
    diag = lax.broadcasted_iota(jnp.int32, (128, 128), 0) == lax.broadcasted_iota(jnp.int32, (128, 128), 1)
    both = (gf[0, 0:128, :] + gf[0, 256:384, :]) + (gf[1, 0:128, :] + gf[1, 256:384, :])
    trace = jnp.sum(jnp.where(diag, both, 0.0), keepdims=True)
    inverse = 1.0 / (jnp.sqrt(trace) + epsilon)
    inverse2 = inverse * inverse

    for chunk in range(R // CHUNK):
        at = slice(chunk * CHUNK, (chunk + 1) * CHUNK)
        squared = dot(gh[at, :], gh[...]) + (dot(gh[at, :], gl[...]) + dot(gl[at, :], gh[...]))
        line = lax.broadcasted_iota(jnp.int32, (CHUNK, R), 0) + chunk * CHUNK
        column = lax.broadcasted_iota(jnp.int32, (CHUNK, R), 1)
        polynomial = jnp.where(line == column, linear_coef, 0.0).astype(F32) + (
            square_coef * gm[at, :] + (quint_coef * squared) * inverse2
        ) * inverse2
        ph[at, :], plo[at, :] = split(polynomial)

    def apply(high, low, vector):
        vh, vl = split(vector)
        wide = dot(high[...], jnp.concatenate([vh, vl], axis=1))
        return wide[:, :COLS] + (wide[:, COLS:] + dot(low[...], vh))

    def apply_second(vector):
        vector = apply(ph, plo, vector)
        vector = apply(gh, gl, vector) * inverse2
        return apply(ph, plo, vector)

    iterate = apply(ph, plo, nest[...] * (inverse * math.sqrt(C)))
    once = apply_second(iterate)
    twice = apply_second(once)
    upd_out[...] = linear_coef * iterate + (square_coef * once + quint_coef * twice)

    momentum_done.wait()
    for copy in sends:
        copy.wait_send()


def finish(mom_ref, upd_ref, mom_out, upd_out, held, sems):
    pairs = ((mom_ref, mom_out), (upd_ref, upd_out))
    loads = [pltpu.make_async_copy(source, held.at[i], sems.at[0, i]) for i, (source, _) in enumerate(pairs)]
    stores = [pltpu.make_async_copy(held.at[i], target, sems.at[1, i]) for i, (_, target) in enumerate(pairs)]
    for load in loads:
        load.start()
    for load, store in zip(loads, stores):
        load.wait()
        store.start()
    for store in stores:
        store.wait()


def local(latents, targets, kv_weight, momentum):
    previous = momentum.reshape(R, COLS)
    dma = pltpu.SemaphoreType.DMA
    any_space = pl.BlockSpec(memory_space=pl.ANY)
    vmem = pl.BlockSpec(memory_space=pltpu.VMEM)
    matrix = jax.ShapeDtypeStruct((R, COLS), F32)
    momentum_new, update = pl.pallas_call(
        kernel,
        out_shape=(matrix, matrix),
        in_specs=[any_space] * 4,
        out_specs=(any_space, vmem),
        scratch_shapes=[
            pltpu.VMEM((CHIPS, 2, QUARTER, R), BF16),
            pltpu.VMEM((CHIPS, 2 * HALF, COLS), BF16),
            pltpu.VMEM((2, CHIPS, HALF, COLS), BF16),
            pltpu.VMEM((2, R, COLS), BF16),
            pltpu.VMEM((2, R, COLS), F32),
            pltpu.VMEM((2, R, COLS), F32),
            pltpu.VMEM((2, R, COLS), F32),
            pltpu.VMEM((2, R, 2 * COLS), BF16),
            pltpu.VMEM((R, COLS), F32),
            pltpu.VMEM((5 * 128, 128), F32),
            pltpu.VMEM((CHIPS - 1, PIECE, 128), F32),
            pltpu.VMEM((PIECE, 128), F32),
            pltpu.VMEM((NZ - 1, PIECE, 128), F32),
            pltpu.VMEM((2, 5 * 128, 128), F32),
            pltpu.VMEM((R, R), F32),
            pltpu.VMEM((R, R), BF16),
            pltpu.VMEM((R, R), BF16),
            pltpu.VMEM((R, R), BF16),
            pltpu.VMEM((R, R), BF16),
            dma((72,)),
            dma((56,)),
            dma((4,)),
            dma((CHIPS,)),
            dma((NX,)),
            dma((NX,)),
            dma,
            dma,
            dma((R // CHUNK, 2)),
            dma,
            dma,
            dma((CHIPS - 1,)),
            dma,
            dma,
            pltpu.SemaphoreType.REGULAR,
        ],
        compiler_params=pltpu.CompilerParams(
            collective_id=0, has_side_effects=True, vmem_limit_bytes=56 << 20
        ),
        name="muon_step",
    )(latents, targets, kv_weight, previous)
    momentum_new, update = pl.pallas_call(
        finish,
        out_shape=(matrix, matrix),
        in_specs=[any_space] * 2,
        out_specs=(any_space, any_space),
        scratch_shapes=[pltpu.VMEM((2, R, COLS), F32), dma((2, 2))],
        name="finish",
    )(momentum_new, update)
    return momentum_new.reshape(R, 1, COLS), update.reshape(R, 1, COLS)


def solution(mesh):
    return jax.shard_map(
        local,
        mesh=mesh,
        in_specs=(P("dp", None), P("dp", "head"), P(None, "head"), P(None, "head", "dp")),
        out_specs=(P(None, "head", "dp"), P(None, "head", "dp")),
        check_vma=False,
    )
```

time: 61.5 us -> 58 us (0.943)
  local copies, waits for them, and re-layouts: 3.34 us -> 0 us
    unnamed x2 -> x0, local copies, waits for them, and re-layouts: 3.34 us -> none
    pallas_call x1 -> x2, Pallas kernels: 57.4 us -> 57.2 us  [the longest x1 55.5 us: local(): pl.pallas_call(kernel, out_shape=(matrix, matrix), in_specs=[any_space] *...]
where the time goes in v3:
time: 58 us; the launch traced here: 57.9 us
  Pallas kernels  57.2 us (99%)
  between operations  0.64 us (1%)
    pallas_call x1, Pallas kernels, local(): pl.pallas_call(kernel, out_shape=(matrix, matrix), in_specs=[any_space] *...  55.5 us
    pallas_call x1, Pallas kernels, local(): pl.pallas_call(finish, out_shape=(matrix, matrix), in_specs=[any_space] *...  1.77 us

profile of v3, /device:TPU:1, one launch (start us, length us, event | category | flops | bytes accessed | tf_op | source)
XLA Modules:
  0.0 57.9 jit_solution(4600641442529179385)
XLA Ops:
  0.6 55.5 %muon_step.1 = (f32[512,128]{1,0:T(8,128)}, f32[512,128]{1,0:T(8,128)}) custom-call(bf16[128,512]{1,0:T(8,128)(2,1)} %lat.1, bf16[128,2048]{1,0:T(8,128)(2,1)} %tgt.1, bf16[512,2048]{1,0:T(8,128)(2,1)} %wgt.1, f32[512,128]{1,0:T(8,128)} %bitcast.7), custom_call_target="tpu_custom_call" | custom-call | tf_op jit(solution)/shard_map/muon_step/pallas_call | solution.py:323
  56.1 1.8 %finish.1 = (f32[512,128]{1,0:T(8,128)}, f32[512,128]{1,0:T(8,128)}) custom-call(f32[512,128]{1,0:T(8,128)} %get-tuple-element.6.mom_ref, f32[512,128]{1,0:T(8,128)} %get-tuple-element.7.upd_ref), custom_call_target="tpu_custom_call" | custom-call | tf_op jit(solution)/shard_map/finish/pallas_call | solution.py:369

commit v4 on v3

--- a/solution.py
+++ b/solution.py
@@ -19,7 +19,7 @@
 HALF = 64
 QUARTER = 32
 CHIPS = NX * NX
-PIECE = 5 * 128 // CHIPS
+PARTS = ((0, 3 * 128), (3 * 128, 2 * 128))
 CHUNK = 256
 
 decay_rate = 0.95
@@ -54,8 +54,8 @@
 
 def kernel(
     lat, tgt, wgt, mom, mom_out, upd_out,
-    lbuf, tstage, tbuf, wbuf, mbuf, gown, gsib, xbuf, nest, gs, rbuf, pz, zbuf, gf, gm, gh, gl, ph, plo,
-    send_a, send_b, local_sem, sem_l, sem_lz, sem_t, sem_w, sem_m, sem_g, sem_r, sem_z, sem_f, sem_s, out_sem, ready,
+    lbuf, tstage, tbuf, wbuf, mbuf, gown, gsib, xbuf, nest, gs, rbuf0, rbuf1, pz0, pz1, zbuf0, zbuf1, gf, gm, gh, gl, ph, plo,
+    send_a, send_b, local_sem, sem_l, sem_lz, sem_t, sem_w, sem_m, sem_g, sem_r, sem_z, sem_f, sem_s, out_sem, ready, ubuf, upd_sem, word,
 ):
     chip = lax.axis_index("dp")
     head = lax.axis_index("head")
@@ -82,12 +82,12 @@
 
     barrier = pltpu.get_barrier_semaphore()
     partners = 1
-    for by in ZRING:
-        pl.semaphore_signal(barrier, inc=1, device_id=along_z(by), device_id_type=MESH)
-        partners += 1
     for _, offset in FAR_FIRST:
         pl.semaphore_signal(barrier, inc=1, device_id=(plane(offset), head), device_id_type=MESH)
         partners += 1
+    for by in (1, NZ - 1):
+        pl.semaphore_signal(barrier, inc=1, device_id=along_z(by), device_id_type=MESH)
+        partners += 1
     pl.semaphore_signal(barrier, inc=1, device_id=sibling, device_id_type=MESH)
 
     zp = lax.rem(z, 2)
@@ -96,18 +96,26 @@
     def quarter(of):
         return lat.at[pl.ds(pl.multiple_of(c * HALF + of * QUARTER, QUARTER), QUARTER)]
 
+    own_quarter = pltpu.make_async_copy(quarter(zp), lbuf.at[chip, zp], local_sem.at[2])
+    own_quarter.start()
     for to in range(CHIPS):
         pltpu.make_async_copy(tgt.at[:, to * COLS : (to + 1) * COLS], tstage.at[to], local_sem.at[0]).start()
     own_weight = pltpu.make_async_copy(wgt.at[:, block_cols], wbuf.at[0], local_sem.at[1])
     own_weight.start()
-    own_quarter = pltpu.make_async_copy(quarter(zp), lbuf.at[chip, zp], local_sem.at[2])
-    own_quarter.start()
     pltpu.make_async_copy(quarter(1 - zp), lbuf.at[chip, 1 - zp], sem_lz.at[x]).start()
     own_momentum = pltpu.make_async_copy(mom, mbuf.at[0], local_sem.at[3])
     own_momentum.start()
     pl.semaphore_wait(barrier, partners)
     pl.semaphore_signal(ready, inc=1, device_id=sibling, device_id_type=MESH)
 
+    def tell_z(turn):
+        pl.semaphore_signal(word.at[turn, 0], inc=1, device_id=along_z(1), device_id_type=MESH)
+        pl.semaphore_signal(word.at[turn, 1], inc=1, device_id=along_z(NZ - 1), device_id_type=MESH)
+
+    def hear_z(turn):
+        pl.semaphore_wait(word.at[turn, 0], 1)
+        pl.semaphore_wait(word.at[turn, 1], 1)
+
     sends = []
     count_a = [0]
 
@@ -117,8 +125,9 @@
         copy.start()
         sends.append(copy)
 
+    own_quarter.wait()
     for _, offset in FAR_FIRST:
-        send_now(quarter(zp), lbuf.at[chip, zp], sem_l.at[chip], (plane(offset), head))
+        send_now(lbuf.at[chip, zp], lbuf.at[chip, zp], sem_l.at[chip], (plane(offset), head))
 
     pltpu.make_async_copy(tstage, tstage, local_sem.at[0]).wait()
     my_rows = pl.ds(pl.multiple_of(c * HALF, HALF), HALF)
@@ -126,6 +135,7 @@
     for _, offset in FAR_FIRST:
         to = plane(offset)
         send_now(tstage.at[to, my_rows], tbuf.at[0, chip], sem_t.at[x], (to, head))
+    tell_z(0)
     pl.semaphore_wait(ready, 1)
     for _, offset in FAR_FIRST:
         to = plane(offset)
@@ -148,7 +158,8 @@
         wait_recv(lbuf.at[slot, zp], sem_l.at[slot])
         swap(slot)
 
-    own_quarter.wait()
+    hear_z(0)
+    tell_z(1)
     wait_recv(wbuf.at[1], sem_w)
     tokens = NX * HALF
 
@@ -174,22 +185,27 @@
                 gown[r] += value
 
     add_gradient(0, residual_of(0), True)
+    hear_z(1)
+    tell_z(2)
     add_gradient(1, residual_of(1), False)
     add_gradient(3, residual_of(3), False)
 
     residual = residual_of(2)
-    for chunk in range(R // CHUNK):
-        at = slice(chunk * CHUNK, (chunk + 1) * CHUNK)
+
+    def chunk_at(of):
+        return pl.ds(pl.multiple_of(of * CHUNK, CHUNK), CHUNK)
+
+    for order, at in enumerate((chunk_at(1 - c), chunk_at(c))):
         part = dot_tn(lbuf[group_of(2), :, :, at].reshape(tokens, CHUNK), residual)
         for r in range(2):
             gown[r, at, :] += part[:, r * COLS : (r + 1) * COLS]
-            send_now(gown.at[r, at], gsib.at[1 - r, at], sem_g.at[chunk, r], sibling)
+            send_now(gown.at[r, at], gsib.at[1 - r, at], sem_g.at[order, r], sibling)
     wait_recv(mbuf.at[1], sem_m)
     own_momentum.wait()
-    for chunk in range(R // CHUNK):
-        at = slice(chunk * CHUNK, (chunk + 1) * CHUNK)
+
+    def nesterov_of(order, at):
         for r in range(2):
-            wait_recv(gsib.at[r, at], sem_g.at[chunk, 1 - r])
+            wait_recv(gsib.at[r, at], sem_g.at[order, 1 - r])
             gradient = (gown[r, at, :] + gsib[r, at, :]) * (1.0 / math.sqrt(TOKENS))
             momentum_new = decay_rate * mbuf[r, at, :] + gradient
             nesterov = gradient + decay_rate * momentum_new
@@ -197,8 +213,6 @@
                 mbuf[0, at, :] = momentum_new
                 nest[at, :] = nesterov
             xbuf[0, at, r * COLS : (r + 1) * COLS], xbuf[1, at, r * COLS : (r + 1) * COLS] = split(nesterov)
-    momentum_done = pltpu.make_async_copy(mbuf.at[0], mom_out, out_sem)
-    momentum_done.start()
 
     def rows(start, size):
         at = pl.ds(pl.multiple_of(start, 128), size)
@@ -208,17 +222,9 @@
         (ah, al), (bh, bl) = a, b
         return dot_nt(ah, bh) + (dot_nt(ah, bl) + dot_nt(al, bh))
 
-    square = rows(c * 256, 256)
-    diagonal = gram(square, square)
-    gs[0:128, :] = diagonal[:128, :128]
-    gs[128:256, :] = diagonal[:128, 128:]
-    gs[256:384, :] = diagonal[128:, 128:]
-    upper = gram(rows(c * 128, 128), rows(256, 256))
-    gs[384:512, :] = upper[:, :128]
-    gs[512:640, :] = upper[:, 128:]
-
-    def piece(of):
-        return pl.ds(pl.multiple_of(of * PIECE, 8), PIECE)
+    def piece(part, of):
+        size = PARTS[part][1] // CHIPS
+        return pl.ds(pl.multiple_of(PARTS[part][0] + of * size, 8), size)
 
     count_b = [0]
 
@@ -228,30 +234,51 @@
         copy.start()
         sends.append(copy)
 
-    for k, offset in FAR_FIRST:
-        to = plane(offset)
-        send_b_now(gs.at[piece(to)], rbuf.at[k], sem_r, (to, head))
-    wait_recv(rbuf, sem_r)
-    total = gs[piece(chip), :]
-    for k in range(CHIPS - 1):
-        total = total + rbuf[k]
-    pz[...] = total
-    for by in ZRING:
-        send_b_now(pz, zbuf.at[by - 1], sem_z, along_z(by))
-    wait_recv(zbuf, sem_z)
-    for k in range(NZ - 1):
-        total = total + zbuf[k]
-    gf[c, piece(chip), :] = total
-    for k, offset in FAR_FIRST:
-        send_b_now(gf.at[c, piece(chip)], gf.at[c, piece(chip)], sem_f.at[k], (plane(offset), head))
-    send_b_now(gf.at[c, piece(chip)], gf.at[c, piece(chip)], sem_s, sibling)
-    for k, offset in enumerate(OFFSETS):
-        source = plane(((4 - offset[0]) % 4, (4 - offset[1]) % 4))
-        wait_recv(gf.at[c, piece(source)], sem_f.at[k])
-        send_b_now(gf.at[c, piece(source)], gf.at[c, piece(source)], sem_s, sibling)
-
-    def place(half):
-        for index, (base, more) in enumerate(BLOCKS):
+    received, summed, over_z = (rbuf0, rbuf1), (pz0, pz1), (zbuf0, zbuf1)
+
+    def scatter(part):
+        for k, offset in FAR_FIRST:
+            to = plane(offset)
+            send_b_now(gs.at[piece(part, to)], received[part].at[k], sem_r.at[part], (to, head))
+
+    hear_z(2)
+    nesterov_of(0, chunk_at(c))
+    square = rows(c * CHUNK, CHUNK)
+    diagonal = gram(square, square)
+    gs[0:128, :] = diagonal[:128, :128]
+    gs[128:256, :] = diagonal[:128, 128:]
+    gs[256:384, :] = diagonal[128:, 128:]
+    scatter(0)
+    nesterov_of(1, chunk_at(1 - c))
+    upper = gram(rows(c * 128, 128), rows(256, 256))
+    gs[384:512, :] = upper[:, :128]
+    gs[512:640, :] = upper[:, 128:]
+    scatter(1)
+    momentum_done = pltpu.make_async_copy(mbuf.at[0], mom_out, out_sem)
+    momentum_done.start()
+
+    for part in range(2):
+        wait_recv(received[part], sem_r.at[part])
+        total = gs[piece(part, chip), :]
+        for k in range(CHIPS - 1):
+            total = total + received[part][k]
+        summed[part][...] = total
+        for by in ZRING:
+            send_b_now(summed[part], over_z[part].at[by - 1], sem_z.at[part], along_z(by))
+    for part in range(2):
+        wait_recv(over_z[part], sem_z.at[part])
+        total = summed[part][...]
+        for k in range(NZ - 1):
+            total = total + over_z[part][k]
+        mine = gf.at[c, piece(part, chip)]
+        gf[c, piece(part, chip), :] = total
+        for k, offset in FAR_FIRST:
+            send_b_now(mine, mine, sem_f.at[part, k], (plane(offset), head))
+        send_b_now(mine, mine, sem_s.at[part], sibling)
+
+    def place(half, part):
+        for index in ((0, 1, 2), (3, 4))[part]:
+            base, more = BLOCKS[index]
             line = pl.ds(pl.multiple_of(base[0] + half * more[0], 128), 128)
             column = pl.ds(pl.multiple_of(base[1] + half * more[1], 128), 128)
             block = gf[half, index * 128 : (index + 1) * 128, :]
@@ -262,9 +289,17 @@
                 gm[column, line] = block
                 gh[column, line], gl[column, line] = split(block)
 
-    place(c)
-    wait_recv(gf.at[1 - c], sem_s)
-    place(1 - c)
+    for part in range(2):
+        for k, offset in enumerate(OFFSETS):
+            source = gf.at[c, piece(part, plane(((4 - offset[0]) % 4, (4 - offset[1]) % 4)))]
+            wait_recv(source, sem_f.at[part, k])
+            send_b_now(source, source, sem_s.at[part], sibling)
+        place(c, part)
+    for part in range(2):
+        start, size = PARTS[part]
+        wait_recv(gf.at[1 - c, start : start + size], sem_s.at[part])
+        place(1 - c, part)
+
     diag = lax.broadcasted_iota(jnp.int32, (128, 128), 0) == lax.broadcasted_iota(jnp.int32, (128, 128), 1)
     both = (gf[0, 0:128, :] + gf[0, 256:384, :]) + (gf[1, 0:128, :] + gf[1, 256:384, :])
     trace = jnp.sum(jnp.where(diag, both, 0.0), keepdims=True)
@@ -294,21 +329,22 @@
     iterate = apply(ph, plo, nest[...] * (inverse * math.sqrt(C)))
     once = apply_second(iterate)
     twice = apply_second(once)
-    upd_out[...] = linear_coef * iterate + (square_coef * once + quint_coef * twice)
-
+    ubuf[...] = linear_coef * iterate + (square_coef * once + quint_coef * twice)
+
+    update_done = pltpu.make_async_copy(ubuf, upd_out, upd_sem)
+    update_done.start()
     momentum_done.wait()
+    update_done.wait()
     for copy in sends:
         copy.wait_send()
 
 
-def finish(mom_ref, upd_ref, mom_out, upd_out, held, sems):
-    pairs = ((mom_ref, mom_out), (upd_ref, upd_out))
-    loads = [pltpu.make_async_copy(source, held.at[i], sems.at[0, i]) for i, (source, _) in enumerate(pairs)]
-    stores = [pltpu.make_async_copy(held.at[i], target, sems.at[1, i]) for i, (_, target) in enumerate(pairs)]
-    for load in loads:
-        load.start()
-    for load, store in zip(loads, stores):
-        load.wait()
+def finish(mom_ref, upd_ref, mom_out, upd_out, sems):
+    stores = [
+        pltpu.make_async_copy(mom_ref, mom_out, sems.at[0]),
+        pltpu.make_async_copy(upd_ref, upd_out, sems.at[1]),
+    ]
+    for store in stores:
         store.start()
     for store in stores:
         store.wait()
@@ -324,7 +360,7 @@
         kernel,
         out_shape=(matrix, matrix),
         in_specs=[any_space] * 4,
-        out_specs=(any_space, vmem),
+        out_specs=(any_space, any_space),
         scratch_shapes=[
             pltpu.VMEM((CHIPS, 2, QUARTER, R), BF16),
             pltpu.VMEM((CHIPS, 2 * HALF, COLS), BF16),
@@ -336,9 +372,9 @@
             pltpu.VMEM((2, R, 2 * COLS), BF16),
             pltpu.VMEM((R, COLS), F32),
             pltpu.VMEM((5 * 128, 128), F32),
-            pltpu.VMEM((CHIPS - 1, PIECE, 128), F32),
-            pltpu.VMEM((PIECE, 128), F32),
-            pltpu.VMEM((NZ - 1, PIECE, 128), F32),
+            *[pltpu.VMEM((CHIPS - 1, size // CHIPS, 128), F32) for _, size in PARTS],
+            *[pltpu.VMEM((size // CHIPS, 128), F32) for _, size in PARTS],
+            *[pltpu.VMEM((NZ - 1, size // CHIPS, 128), F32) for _, size in PARTS],
             pltpu.VMEM((2, 5 * 128, 128), F32),
             pltpu.VMEM((R, R), F32),
             pltpu.VMEM((R, R), BF16),
@@ -346,32 +382,36 @@
             pltpu.VMEM((R, R), BF16),
             pltpu.VMEM((R, R), BF16),
             dma((72,)),
-            dma((56,)),
+            dma((112,)),
             dma((4,)),
             dma((CHIPS,)),
             dma((NX,)),
             dma((NX,)),
             dma,
             dma,
-            dma((R // CHUNK, 2)),
-            dma,
-            dma,
-            dma((CHIPS - 1,)),
-            dma,
+            dma((2, 2)),
+            dma((2,)),
+            dma((2,)),
+            dma((2, CHIPS - 1)),
+            dma((2,)),
             dma,
             pltpu.SemaphoreType.REGULAR,
+            pltpu.VMEM((R, COLS), F32),
+            dma,
+            pltpu.SemaphoreType.REGULAR((3, 2)),
         ],
         compiler_params=pltpu.CompilerParams(
-            collective_id=0, has_side_effects=True, vmem_limit_bytes=56 << 20
+            collective_id=0, has_side_effects=True, vmem_limit_bytes=32 << 20
         ),
         name="muon_step",
-    )(latents, targets, kv_weight, previous)
+    )(*[pltpu.with_memory_space_constraint(v, pltpu.HBM) for v in (latents, targets, kv_weight, previous)])
     momentum_new, update = pl.pallas_call(
         finish,
         out_shape=(matrix, matrix),
-        in_specs=[any_space] * 2,
+        in_specs=[vmem] * 2,
         out_specs=(any_space, any_space),
-        scratch_shapes=[pltpu.VMEM((2, R, COLS), F32), dma((2, 2))],
+        scratch_shapes=[dma((2,))],
+        compiler_params=pltpu.CompilerParams(vmem_limit_bytes=4 << 20),
         name="finish",
     )(momentum_new, update)
     return momentum_new.reshape(R, 1, COLS), update.reshape(R, 1, COLS)

time: 58 us -> 54.5 us (0.940)
  Pallas kernels: 57.2 us -> 53.8 us
    pallas_call x1, Pallas kernels: 55.5 us -> 53 us  [local(): pl.pallas_call(kernel, out_shape=(matrix, matrix), in_specs=[any_space] *...]
    pallas_call x1, Pallas kernels: 1.77 us -> 0.81 us  [local(): pl.pallas_call(finish, out_shape=(matrix, matrix), in_specs=[vmem] * 2, o...]
where the time goes in v4:
time: 54.5 us; the launch traced here: 54.4 us
  Pallas kernels  53.8 us (99%)
  between operations  0.64 us (1%)
    pallas_call x1, Pallas kernels, local(): pl.pallas_call(kernel, out_shape=(matrix, matrix), in_specs=[any_space] *...  53 us

profile of v4, /device:TPU:1, one launch (start us, length us, event | category | flops | bytes accessed | tf_op | source)
XLA Modules:
  0.0 54.4 jit_solution(17488951205824781614)
XLA Ops:
  0.6 53.0 %muon_step.1 = (f32[512,128]{1,0:T(8,128)S(1)}, f32[512,128]{1,0:T(8,128)S(1)}) custom-call(bf16[128,512]{1,0:T(8,128)(2,1)} %lat.1, bf16[128,2048]{1,0:T(8,128)(2,1)} %tgt.1, bf16[512,2048]{1,0:T(8,128)(2,1)} %wgt.1, f32[512,128]{1,0:T(8,128)} %bitcast.7), custom_call_target="tpu_custom_call" | custom-call | tf_op jit(solution)/shard_map/muon_step/pallas_call | solution.py:359
  53.6 0.8 %finish.1 = (f32[512,128]{1,0:T(8,128)}, f32[512,128]{1,0:T(8,128)}) custom-call(f32[512,128]{1,0:T(8,128)S(1)} %get-tuple-element.6.mom_ref, f32[512,128]{1,0:T(8,128)S(1)} %get-tuple-element.7.upd_ref), custom_call_target="tpu_custom_call" | custom-call | tf_op jit(solution)/shard_map/finish/pallas_call | solution.py:408

commit v5 on v4

--- a/solution.py
+++ b/solution.py
@@ -30,6 +30,7 @@
 
 OFFSETS = [(0, 1), (0, 3), (1, 0), (3, 0), (1, 1), (1, 3), (3, 1), (3, 3), (0, 2), (2, 0), (1, 2), (3, 2), (2, 1), (2, 3), (2, 2)]
 FAR_FIRST = list(reversed(list(enumerate(OFFSETS))))
+DIRECT = ((0, 2), (2, 0), (0, 1), (0, 3), (1, 0), (3, 0))
 RING = (1, 3, 2)
 ZRING = (4, 3, 5, 2, 6, 1, 7)
 BLOCKS = (((0, 0), (256, 256)), ((0, 128), (256, 256)), ((128, 128), (256, 256)), ((0, 256), (128, 0)), ((0, 384), (128, 0)))
@@ -55,7 +56,7 @@
 def kernel(
     lat, tgt, wgt, mom, mom_out, upd_out,
     lbuf, tstage, tbuf, wbuf, mbuf, gown, gsib, xbuf, nest, gs, rbuf0, rbuf1, pz0, pz1, zbuf0, zbuf1, gf, gm, gh, gl, ph, plo,
-    send_a, send_b, local_sem, sem_l, sem_lz, sem_t, sem_w, sem_m, sem_g, sem_r, sem_z, sem_f, sem_s, out_sem, ready, ubuf, upd_sem, word,
+    send_a, send_b, local_sem, sem_l, sem_lz, sem_t, sem_w, sem_m, sem_g, sem_r, sem_z, sem_f, sem_s, out_sem, ready, word,
 ):
     chip = lax.axis_index("dp")
     head = lax.axis_index("head")
@@ -71,6 +72,11 @@
 
     def plane(offset):
         return step(x, offset[0]) * NX + step(y, offset[1])
+
+    def turned(offset):
+        a = jnp.where(c == 0, offset[0], offset[1])
+        b = jnp.where(c == 0, offset[1], offset[0])
+        return plane((a, b))
 
     def remote(src, dst, ssem, rsem, device):
         return pltpu.make_async_remote_copy(
@@ -126,12 +132,38 @@
         sends.append(copy)
 
     own_quarter.wait()
-    for _, offset in FAR_FIRST:
-        send_now(lbuf.at[chip, zp], lbuf.at[chip, zp], sem_l.at[chip], (plane(offset), head))
+    for offset in DIRECT:
+        send_now(lbuf.at[chip, zp], lbuf.at[chip, zp], sem_l.at[chip], (turned(offset), head))
 
     pltpu.make_async_copy(tstage, tstage, local_sem.at[0]).wait()
     my_rows = pl.ds(pl.multiple_of(c * HALF, HALF), HALF)
     sib_rows = pl.ds(pl.multiple_of((1 - c) * HALF, HALF), HALF)
+    own_weight.wait()
+    send_now(wbuf.at[0], wbuf.at[1], sem_w, sibling)
+    send_now(tstage.at[chip, sib_rows], tbuf.at[1, chip], sem_t.at[x], sibling)
+    send_now(mom, mbuf.at[1], sem_m, sibling)
+    pltpu.make_async_copy(tstage.at[chip, my_rows], tbuf.at[0, chip], sem_t.at[x]).start()
+
+    flip = [0]
+
+    def swap(slot):
+        side = 1 if flip[0] % 2 == 0 else NZ - 1
+        flip[0] += 1
+        send_now(lbuf.at[slot, zp], lbuf.at[slot, zp], sem_lz.at[lax.div(slot, NX)], along_z(side))
+
+    def arrival(offset, passed_to=()):
+        slot = turned(offset)
+        wait_recv(lbuf.at[slot, zp], sem_l.at[slot])
+        for onward in passed_to:
+            send_now(lbuf.at[slot, zp], lbuf.at[slot, zp], sem_l.at[slot], (turned(onward), head))
+        swap(slot)
+
+    arrival((0, 1), ((1, 0), (3, 0)))
+    arrival((0, 3), ((1, 0), (3, 0)))
+    arrival((0, 2), ((2, 0), (1, 0), (3, 0)))
+    arrival((2, 0), ((0, 1), (0, 3)))
+    arrival((1, 0))
+    arrival((3, 0))
     for _, offset in FAR_FIRST:
         to = plane(offset)
         send_now(tstage.at[to, my_rows], tbuf.at[0, chip], sem_t.at[x], (to, head))
@@ -140,23 +172,8 @@
     for _, offset in FAR_FIRST:
         to = plane(offset)
         send_now(tstage.at[to, sib_rows], tbuf.at[1, chip], sem_t.at[x], (to, z * 2 + (1 - c)))
-    own_weight.wait()
-    send_now(wbuf.at[0], wbuf.at[1], sem_w, sibling)
-    send_now(tstage.at[chip, sib_rows], tbuf.at[1, chip], sem_t.at[x], sibling)
-    send_now(mom, mbuf.at[1], sem_m, sibling)
-    pltpu.make_async_copy(tstage.at[chip, my_rows], tbuf.at[0, chip], sem_t.at[x]).start()
-
-    flip = [0]
-
-    def swap(slot):
-        side = 1 if flip[0] % 2 == 0 else NZ - 1
-        flip[0] += 1
-        send_now(lbuf.at[slot, zp], lbuf.at[slot, zp], sem_lz.at[lax.div(slot, NX)], along_z(side))
-
-    for offset in OFFSETS:
-        slot = plane(offset)
-        wait_recv(lbuf.at[slot, zp], sem_l.at[slot])
-        swap(slot)
+    for offset in OFFSETS[4:8] + OFFSETS[10:]:
+        arrival(offset)
 
     hear_z(0)
     tell_z(1)
@@ -329,12 +346,9 @@
     iterate = apply(ph, plo, nest[...] * (inverse * math.sqrt(C)))
     once = apply_second(iterate)
     twice = apply_second(once)
-    ubuf[...] = linear_coef * iterate + (square_coef * once + quint_coef * twice)
-
-    update_done = pltpu.make_async_copy(ubuf, upd_out, upd_sem)
-    update_done.start()
+    upd_out[...] = linear_coef * iterate + (square_coef * once + quint_coef * twice)
+
     momentum_done.wait()
-    update_done.wait()
     for copy in sends:
         copy.wait_send()
 
@@ -360,7 +374,7 @@
         kernel,
         out_shape=(matrix, matrix),
         in_specs=[any_space] * 4,
-        out_specs=(any_space, any_space),
+        out_specs=(any_space, vmem),
         scratch_shapes=[
             pltpu.VMEM((CHIPS, 2, QUARTER, R), BF16),
             pltpu.VMEM((CHIPS, 2 * HALF, COLS), BF16),
@@ -396,8 +410,6 @@
             dma((2,)),
             dma,
             pltpu.SemaphoreType.REGULAR,
-            pltpu.VMEM((R, COLS), F32),
-            dma,
             pltpu.SemaphoreType.REGULAR((3, 2)),
         ],
         compiler_params=pltpu.CompilerParams(

time: 54.5 us -> 52.3 us (0.960)
  Pallas kernels: 53.8 us -> 51.6 us
    pallas_call x1, Pallas kernels: 53 us -> 50.8 us  [local(): pl.pallas_call(kernel, out_shape=(matrix, matrix), in_specs=[any_space] *...]
where the time goes in v5:
time: 52.3 us; the launch traced here: 52.2 us
  Pallas kernels  51.6 us (99%)
  between operations  0.64 us (1%)
    pallas_call x1, Pallas kernels, local(): pl.pallas_call(kernel, out_shape=(matrix, matrix), in_specs=[any_space] *...  50.8 us

profile of v5, /device:TPU:1, one launch (start us, length us, event | category | flops | bytes accessed | tf_op | source)
XLA Modules:
  0.0 52.2 jit_solution(5942310065357134192)
XLA Ops:
  0.6 50.8 %muon_step.1 = (f32[512,128]{1,0:T(8,128)S(1)}, f32[512,128]{1,0:T(8,128)S(1)}) custom-call(bf16[128,512]{1,0:T(8,128)(2,1)} %lat.1, bf16[128,2048]{1,0:T(8,128)(2,1)} %tgt.1, bf16[512,2048]{1,0:T(8,128)(2,1)} %wgt.1, f32[512,128]{1,0:T(8,128)} %bitcast.7), custom_call_target="tpu_custom_call" | custom-call | tf_op jit(solution)/shard_map/muon_step/pallas_call | solution.py:373
  51.4 0.8 %finish.1 = (f32[512,128]{1,0:T(8,128)}, f32[512,128]{1,0:T(8,128)}) custom-call(f32[512,128]{1,0:T(8,128)S(1)} %get-tuple-element.6.mom_ref, f32[512,128]{1,0:T(8,128)S(1)} %get-tuple-element.7.upd_ref), custom_call_target="tpu_custom_call" | custom-call | tf_op jit(solution)/shard_map/finish/pallas_call | solution.py:420

commit v6 on v5

--- a/solution.py
+++ b/solution.py
@@ -124,6 +124,10 @@
 
     sends = []
     count_a = [0]
+
+    def drain():
+        while sends:
+            sends.pop(0).wait_send()
 
     def send_now(src, dst, rsem, device):
         copy = remote(src, dst, send_a.at[count_a[0]], rsem, device)
@@ -274,6 +278,7 @@
     momentum_done = pltpu.make_async_copy(mbuf.at[0], mom_out, out_sem)
     momentum_done.start()
 
+    drain()
     for part in range(2):
         wait_recv(received[part], sem_r.at[part])
         total = gs[piece(part, chip), :]
@@ -282,6 +287,7 @@
         summed[part][...] = total
         for by in ZRING:
             send_b_now(summed[part], over_z[part].at[by - 1], sem_z.at[part], along_z(by))
+    drain()
     for part in range(2):
         wait_recv(over_z[part], sem_z.at[part])
         total = summed[part][...]
@@ -292,6 +298,8 @@
         for k, offset in FAR_FIRST:
             send_b_now(mine, mine, sem_f.at[part, k], (plane(offset), head))
         send_b_now(mine, mine, sem_s.at[part], sibling)
+
+    drain()
 
     def place(half, part):
         for index in ((0, 1, 2), (3, 4))[part]:
@@ -312,6 +320,7 @@
             wait_recv(source, sem_f.at[part, k])
             send_b_now(source, source, sem_s.at[part], sibling)
         place(c, part)
+    drain()
     for part in range(2):
         start, size = PARTS[part]
         wait_recv(gf.at[1 - c, start : start + size], sem_s.at[part])
@@ -349,8 +358,6 @@
     upd_out[...] = linear_coef * iterate + (square_coef * once + quint_coef * twice)
 
     momentum_done.wait()
-    for copy in sends:
-        copy.wait_send()
 
 
 def finish(mom_ref, upd_ref, mom_out, upd_out, sems):

time: 52.3 us -> 52 us (level)
  no operation moved by 1% of the time
where the time goes in v6:
time: 52 us
  Pallas kernels  51.3 us (99%)
  between operations  0.64 us (1%)
    pallas_call x1, Pallas kernels, local(): pl.pallas_call(kernel, out_shape=(matrix, matrix), in_specs=[any_space] *...  50.5 us

profile of v6, /device:TPU:1, one launch (start us, length us, event | category | flops | bytes accessed | tf_op | source)
XLA Modules:
  0.0 52.0 jit_solution(16876436963937534355)
XLA Ops:
  0.6 50.5 %muon_step.1 = (f32[512,128]{1,0:T(8,128)S(1)}, f32[512,128]{1,0:T(8,128)S(1)}) custom-call(bf16[128,512]{1,0:T(8,128)(2,1)} %lat.1, bf16[128,2048]{1,0:T(8,128)(2,1)} %tgt.1, bf16[512,2048]{1,0:T(8,128)(2,1)} %wgt.1, f32[512,128]{1,0:T(8,128)} %bitcast.7), custom_call_target="tpu_custom_call" | custom-call | tf_op jit(solution)/shard_map/muon_step/pallas_call | solution.py:380
  51.1 0.8 %finish.1 = (f32[512,128]{1,0:T(8,128)}, f32[512,128]{1,0:T(8,128)}) custom-call(f32[512,128]{1,0:T(8,128)S(1)} %get-tuple-element.6.mom_ref, f32[512,128]{1,0:T(8,128)S(1)} %get-tuple-element.7.upd_ref), custom_call_target="tpu_custom_call" | custom-call | tf_op jit(solution)/shard_map/finish/pallas_call | solution.py:427
